TPU v7x, 32 devices: a whole 2x2x4 slice. The times are simulated.
32 devices in a mesh: tm: 8 (over y, x, core), cuts: 4 (over z).
Axes of the slice: x: 2, y: 2, z: 4, core: 2. Of those that a mesh axis runs over, the one named last changes fastest.
Arguments:
- volume: float32 [16, 32, 24, 1024], P('tm', 'cuts'), may hold values from -6 to 6
- measured: bfloat16 [16, 6, 32, 24, 1024], P('tm', None, 'cuts'), may hold values from -6 to 6
- counts: int32 [16], P('tm'), may hold values from 2 to 6, as said below
- vshift: int32 [16, 6], P('tm'), may hold values from -2 to 2, as said below
- hshift: int32 [16, 6], P('tm'), may hold values from -16 to 16
- angles: int32 [16, 6], P('tm'), may hold values from 0 to 3
- blocks: bfloat16 [4, 1024, 1024], replicated, may hold values from -0.1875 to 0.1875
Outputs:
- gradient: float32 [16, 32, 24, 1024], P('tm', 'cuts')
Inputs may be any that keep to these rules, and one draw needn't show every extreme that they name: `counts`: some frame has exactly 2 live views and another exactly 6. `vshift`: some live view has the shift 2 and another -2.
All inputs are finite; a program needn't handle non-finite values.
Results may differ from a plain program's by a relative error of at most 0.0029.
Values may be sent and summed in bfloat16 or wider, within the bound.
A program may use at most 64 MiB of HBM per device.

v0:
```python
from functools import partial

import jax
import jax.numpy as jnp
from jax import lax
from jax.experimental import pallas as pl
from jax.experimental.pallas import tpu as pltpu
from jax.sharding import PartitionSpec as P

H = 2
LANES = 128
NT = (((1,), (1,)), ((), ()))
MESH = pl.DeviceIdType.MESH


def lateral(x, by):
    columns = x.shape[1] // LANES
    lane = lax.broadcasted_iota(jnp.int32, (x.shape[0], LANES), 1)
    take_next, take_last = lane >= LANES - by, lane < -by
    amount = lax.rem(LANES - by, LANES)
    zero = jnp.zeros((x.shape[0], LANES), x.dtype)
    turned = [pltpu.roll(x[:, c * LANES : (c + 1) * LANES], amount, 1) for c in range(columns)]
    turned = [zero] + turned + [zero]
    return [
        jnp.where(take_next, turned[c + 2], jnp.where(take_last, turned[c], turned[c + 1]))
        for c in range(columns)
    ]


def ordered(count, kind_of, kinds, views):
    keys = [jnp.where(v < count, kind_of[v], kinds) for v in range(views)]
    ranks = []
    for v in range(views):
        rank = jnp.int32(0)
        for u in range(views):
            if u != v:
                ahead = keys[u] <= keys[v] if u < v else keys[u] < keys[v]
                rank = rank + jnp.where(ahead, 1, 0)
        ranks.append(rank)
    view_at, key_at = [], []
    for j in range(views):
        view, key = jnp.int32(0), jnp.int32(0)
        for v in range(views):
            view = view + jnp.where(ranks[v] == j, v, 0)
            key = key + jnp.where(ranks[v] == j, keys[v], 0)
        view_at.append(view)
        key_at.append(key)
    return view_at, key_at


def kernel(
    seen_count, counts, vshift, hshift, angles, volume_in, measured_in, blocks_in, out, *scratch
):
    seen = scratch[:seen_count]
    compute(
        seen, counts, vshift, hshift, angles, volume_in, measured_in, blocks_in, out, *scratch[seen_count:]
    )


def compute(
    seen, counts, vshift, hshift, angles, volume_in, measured_in, blocks_in, out,
    volume, blocks, low, sums, ways, image, terms, rim_rows, rim_fit,
    up, down, below, above, before, after, load_sem, block_sem, send_sem, recv_sem,
):
    frames, views, slices, height, width = measured_in.shape
    kinds = blocks_in.shape[0]
    rows, rim = slices * height, H * height
    wide = slices + 2 * H
    slab, cuts = lax.axis_index("cuts"), lax.axis_size("cuts")
    time, times = lax.axis_index("tm"), lax.axis_size("tm")
    has_below, has_above = slab > 0, slab + 1 < cuts
    has_before, has_after = time > 0, time + 1 < times
    next_slab, last_slab = lax.rem(slab + 1, cuts), lax.rem(slab + cuts - 1, cuts)
    next_time, last_time = lax.rem(time + 1, times), lax.rem(time + times - 1, times)

    get_volume = pltpu.make_async_copy(volume_in, volume, load_sem.at[0])
    get_volume.start()

    def get_block(a):
        return pltpu.make_async_copy(blocks_in.at[a], blocks.at[a], block_sem.at[a])

    get_block(0).start()
    blank = jnp.zeros((2 * H, height, width), seen[0].dtype)
    get_seen = []
    for f in range(frames):
        for v in range(views):
            seen[f][v, : 2 * H] = blank
            seen[f][v, 2 * H + slices :] = blank
        get_seen.append(
            pltpu.make_async_copy(
                measured_in.at[f], seen[f].at[:, pl.ds(2 * H, slices)], load_sem.at[1 + f]
            )
        )
        get_seen[f].start()
        if f + 1 < kinds:
            get_block(f + 1).start()
    for a in range(frames + 1, kinds):
        get_block(a).start()
    barrier = pltpu.get_barrier_semaphore()
    neighbours = (
        (has_below, {"cuts": last_slab}),
        (has_above, {"cuts": next_slab}),
        (has_before, {"tm": last_time}),
        (has_after, {"tm": next_time}),
    )
    for there, device in neighbours:

        @pl.when(there)
        def _():
            pl.semaphore_signal(barrier, inc=1, device_id=device, device_id_type=MESH)

    for f in range(frames):
        sums[views, f] = jnp.zeros(sums.shape[2:], sums.dtype)
        ways[views, f] = jnp.zeros(ways.shape[2:], ways.dtype)
    for there, ref in ((has_below, below), (has_above, above), (has_before, before), (has_after, after)):

        @pl.when(jnp.logical_not(there))
        def _():
            ref[...] = jnp.zeros(ref.shape, ref.dtype)

    get_volume.wait()
    for f in range(frames):
        low[f * rows : (f + 1) * rows] = volume[f].astype(low.dtype)

    pl.semaphore_wait(barrier, sum(jnp.where(there, 1, 0) for there, _ in neighbours))

    def remote(src, dst, n, device):
        return pltpu.make_async_remote_copy(
            src_ref=src,
            dst_ref=dst,
            send_sem=send_sem.at[n],
            recv_sem=recv_sem.at[n],
            device_id=device,
            device_id_type=MESH,
        )

    transfers = (
        (remote(low.at[pl.ds((frames - 1) * rows, rows)], before, 0, {"tm": next_time}), has_after, has_before),
        (remote(low.at[pl.ds(0, rows)], after, 1, {"tm": last_time}), has_before, has_after),
        (remote(up, below, 2, {"cuts": next_slab}), has_above, has_below),
        (remote(down, above, 3, {"cuts": last_slab}), has_below, has_above),
    )

    def begin(transfer):
        copy, sends, _ = transfer

        @pl.when(sends)
        def _():
            copy.start()

    begin(transfers[0])
    begin(transfers[1])
    share = kinds // frames
    part = wide // share

    for f in range(frames):
        view_at, key_at = ordered(
            counts[f], [angles[f, v] for v in range(views)], kinds, views
        )
        vertical, side = [vshift[f, v] for v in view_at], [hshift[f, v] for v in view_at]
        same = [
            jnp.where(key_at[j] == key_at[j - 1], 1, 0).astype(jnp.float32) for j in range(1, views)
        ]
        for j in range(views):
            z = lax.broadcasted_iota(jnp.int32, (slices, width), 0) + (slab * slices - vertical[j])
            e = lax.broadcasted_iota(jnp.int32, (slices, width), 1) + side[j]
            inside = (z >= 0) & (z < cuts * slices) & (e >= 0) & (e < width)
            inside = jnp.where(inside, 1.0, 0.0)
            ways[j, f] = inside if j == 0 else inside + same[j - 1] * ways[j - 1, f]
        get_seen[f].wait()

        def add_slice(z):
            for j in range(views):
                x = seen[f][view_at[j], z + H - vertical[j]].astype(jnp.float32)
                for c, y in enumerate(lateral(x, side[j])):
                    lanes = pl.ds(c * LANES, LANES)
                    if j > 0:
                        y = y + same[j - 1] * sums[j - 1, f, z, :, lanes]
                    sums[j, f, z, :, lanes] = y

        def project(k, carry):
            a = f * share + k
            get_block(a).wait()
            for q in range(2):
                lanes = pl.ds(q * width // 2, width // 2)
                image[a, :, lanes] = jnp.dot(
                    low[...], blocks[a, :, lanes], preferred_element_type=jnp.float32
                )
                for i in range(q * part // 2, (q + 1) * part // 2):
                    add_slice(k * part + i)
            return carry

        lax.fori_loop(0, share, project, 0)

    def slot_of(f, a):
        upto, here = jnp.int32(0), jnp.int32(0)
        for v in range(views):
            live = v < counts[f]
            upto = upto + jnp.where(jnp.logical_and(live, angles[f, v] <= a), 1, 0)
            here = here + jnp.where(jnp.logical_and(live, angles[f, v] == a), 1, 0)
        return jnp.where(here > 0, upto - 1, views)

    def rims(a, carry):
        for f in range(frames):
            slot = slot_of(f, a)
            for i in range(H):
                at = f * rim + i * height
                rim_rows[at : at + height] = sums[slot, f, H + slices + i].astype(rim_rows.dtype)
                at += frames * rim
                rim_rows[at : at + height] = sums[slot, f, i].astype(rim_rows.dtype)
        rim_fit[...] += lax.dot_general(rim_rows[...], blocks[a], NT, preferred_element_type=jnp.float32)
        return carry

    rim_fit[...] = jnp.zeros_like(rim_fit)
    lax.fori_loop(0, kinds, rims, 0)
    for f in range(frames):
        up[f] = rim_fit[f * rim : (f + 1) * rim].astype(up.dtype)
        down[f] = rim_fit[(frames + f) * rim : (frames + f + 1) * rim].astype(down.dtype)
        out[f] = jnp.zeros(out.shape[1:], out.dtype)
    begin(transfers[2])
    begin(transfers[3])

    def end(transfer):
        copy, sends, takes = transfer

        @pl.when(sends)
        def _():
            copy.wait_send()

        @pl.when(takes)
        def _():
            copy.wait_recv()

    end(transfers[0])
    end(transfers[1])
    first_factor = jnp.where(has_before, 0.5, 0.0).astype(jnp.float32)
    last_factor = jnp.where(has_after, 0.5, 0.0).astype(jnp.float32)
    stripe = rows // kinds

    def smooth(a):
        part = pl.ds(pl.multiple_of(a * stripe, stripe), stripe)
        held = [before[part].astype(jnp.float32)] + [volume[f, part] for f in range(frames)]
        held += [after[part].astype(jnp.float32)]
        weights = []
        for f in range(frames + 1):
            differ = held[f + 1] - held[f]
            weights.append(differ * lax.rsqrt(differ * differ + 0.25))
        for f in range(frames):
            ahead = first_factor if f == 0 else 0.5
            behind = last_factor if f == frames - 1 else 0.5
            out[f, part] += ahead * weights[f] - behind * weights[f + 1]

    def main(a, carry):
        for f in range(frames):
            slot = slot_of(f, a)
            for z in range(slices):
                at = f * rows + z * height
                way = ways[slot, f, z : z + 1, :]
                term = way * image[a, at : at + height] - sums[slot, f, H + z]
                terms[at : at + height] = term.astype(terms.dtype)
        back = lax.dot_general(terms[...], blocks[a], NT, preferred_element_type=jnp.float32)
        for f in range(frames):
            out[f] += back[f * rows : (f + 1) * rows]

        smooth(a)
        return carry

    lax.fori_loop(0, kinds, main, 0)

    end(transfers[2])
    end(transfers[3])
    for f in range(frames):
        out[f, :rim] -= below[f].astype(jnp.float32)
        out[f, rows - rim :] -= above[f].astype(jnp.float32)


def body(volume, measured, counts, vshift, hshift, angles, blocks):
    frames, slices, height, width = volume.shape
    views, kinds = measured.shape[1], blocks.shape[0]
    rows, rim = slices * height, H * height
    smem = pl.BlockSpec(memory_space=pltpu.SMEM)
    anywhere = pl.BlockSpec(memory_space=pl.ANY)
    low_type, wide_type = jnp.bfloat16, jnp.float32
    out = pl.pallas_call(
        partial(kernel, frames),
        in_specs=[smem] * 4 + [anywhere] * 3,
        out_specs=pl.BlockSpec(memory_space=pltpu.VMEM),
        out_shape=jax.ShapeDtypeStruct((frames, rows, width), wide_type),
        scratch_shapes=[pltpu.VMEM((views, slices + 4 * H, height, width), low_type)] * frames
        + [
            pltpu.VMEM((frames, rows, width), wide_type),
            pltpu.VMEM((kinds, width, width), low_type),
            pltpu.VMEM((frames * rows, width), low_type),
            pltpu.VMEM((views + 1, frames, slices + 2 * H, height, width), wide_type),
            pltpu.VMEM((views + 1, frames, slices, width), wide_type),
            pltpu.VMEM((kinds, frames * rows, width), wide_type),
            pltpu.VMEM((frames * rows, width), low_type),
            pltpu.VMEM((2 * frames * rim, width), low_type),
            pltpu.VMEM((2 * frames * rim, width), wide_type),
        ]
        + [pltpu.VMEM((frames, rim, width), low_type)] * 4
        + [pltpu.VMEM((rows, width), low_type)] * 2
        + [
            pltpu.SemaphoreType.DMA((1 + frames,)),
            pltpu.SemaphoreType.DMA((kinds,)),
            pltpu.SemaphoreType.DMA((4,)),
            pltpu.SemaphoreType.DMA((4,)),
        ],
        compiler_params=pltpu.CompilerParams(
            collective_id=0, has_side_effects=True, vmem_limit_bytes=60 * 2**20
        ),
        name="gradient",
    )(
        counts,
        vshift,
        hshift,
        angles,
        volume.reshape(frames, rows, width),
        measured,
        blocks,
    )
    return out.reshape(frames, slices, height, width)


def solution(mesh):
    in_specs = (
        P("tm", "cuts", None, None),
        P("tm", None, "cuts", None, None),
        P("tm"),
        P("tm", None),
        P("tm", None),
        P("tm", None),
        P(),
    )
    out_specs = P("tm", "cuts", None, None)
    return jax.shard_map(body, mesh=mesh, in_specs=in_specs, out_specs=out_specs, check_vma=False)
```

profile of v0, /device:TPU:0, one launch (start us, length us, event | category | flops | bytes accessed | tf_op | source)
XLA Modules:
  0.0 25.2 jit_solution(15150784479230761171)
XLA Ops:
  0.0 22.5 %gradient.1 = f32[2,192,1024]{2,1,0:T(8,128)} custom-call(s32[2]{0:T(128)} %counts.1, s32[2,6]{1,0:T(2,128)} %vshift.1, s32[2,6]{1,0:T(2,128)} %hshift.1, s32[2,6]{1,0:T(2,128)} %angles.1, f32[2,192,1024]{2,1,0:T(8,128)} %bitcast.3, bf16[2,6,8,24,1024]{4,3,2,1,0:T(8,128)(2,1)} %measured_in.1, bf16[4,1024,1024]{2,1,0:T(8,128)(2,1)} %blocks_in.1), custom_call_target="tpu_custom_call" | custom-call | tf_op jit(solution)/shard_map/gradient/pallas_call | solution.py:284
  22.5 2.7 %copy.9 = f32[2,8,24,1024]{3,2,1,0:T(8,128)} copy(f32[2,8,24,1024]{3,2,1,0:T(8,128)} %bitcast.2) | data formatting | bytes 3145728
where the time goes:
time: 25.4 us; the launch traced here: 25.2 us
  Pallas kernels  22.5 us (89%)
  local copies, waits for them, and re-layouts  2.73 us (11%)
    pallas_call x1, Pallas kernels, body(): pl.pallas_call(partial(kernel, frames), in_specs=[smem] * 4 + [anywhere]...  22.5 us
    unnamed x1, local copies, waits for them, and re-layouts  2.73 us

commit v1 on v0

--- a/solution.py
+++ b/solution.py
@@ -285,7 +285,7 @@
         partial(kernel, frames),
         in_specs=[smem] * 4 + [anywhere] * 3,
         out_specs=pl.BlockSpec(memory_space=pltpu.VMEM),
-        out_shape=jax.ShapeDtypeStruct((frames, rows, width), wide_type),
+        out_shape=pltpu.VMEM((frames, rows, width), wide_type),
         scratch_shapes=[pltpu.VMEM((views, slices + 4 * H, height, width), low_type)] * frames
         + [
             pltpu.VMEM((frames, rows, width), wide_type),
@@ -307,7 +307,7 @@
             pltpu.SemaphoreType.DMA((4,)),
         ],
         compiler_params=pltpu.CompilerParams(
-            collective_id=0, has_side_effects=True, vmem_limit_bytes=60 * 2**20
+            collective_id=0, has_side_effects=True, vmem_limit_bytes=61 * 2**20
         ),
         name="gradient",
     )(

time: 25.4 us -> 22.6 us (0.89)
  local copies, waits for them, and re-layouts: 2.73 us -> 1.15 us
  Pallas kernels: 22.5 us -> 21.3 us
    unnamed x1, local copies, waits for them, and re-layouts: 2.73 us -> 1.15 us
    pallas_call x1, Pallas kernels: 22.5 us -> 21.3 us  [body(): pl.pallas_call(partial(kernel, frames), in_specs=[smem] * 4 + [anywhere]...]
where the time goes in v1:
time: 22.6 us; the launch traced here: 22.5 us
  Pallas kernels  21.3 us (94%)
  local copies, waits for them, and re-layouts  1.15 us (5%)
    pallas_call x1, Pallas kernels, body(): pl.pallas_call(partial(kernel, frames), in_specs=[smem] * 4 + [anywhere]...  21.3 us
    unnamed x1, local copies, waits for them, and re-layouts  1.15 us

profile of v1, /device:TPU:0, one launch (start us, length us, event | category | flops | bytes accessed | tf_op | source)
XLA Modules:
  0.0 22.5 jit_solution(2412147626804243064)
XLA Ops:
  0.0 21.3 %gradient.1 = f32[2,192,1024]{2,1,0:T(8,128)S(1)} custom-call(s32[2]{0:T(128)} %counts.1, s32[2,6]{1,0:T(2,128)} %vshift.1, s32[2,6]{1,0:T(2,128)} %hshift.1, s32[2,6]{1,0:T(2,128)} %angles.1, f32[2,192,1024]{2,1,0:T(8,128)} %bitcast.3, bf16[2,6,8,24,1024]{4,3,2,1,0:T(8,128)(2,1)} %measured_in.1, bf16[4,1024,1024]{2,1,0:T(8,128)(2,1)} %blocks_in.1), custom_call_target="tpu_custom_call" | custom-call | tf_op jit(solution)/shard_map/gradient/pallas_call | solution.py:284
  21.3 1.1 %copy.9 = f32[2,8,24,1024]{3,2,1,0:T(8,128)} copy(f32[2,8,24,1024]{3,2,1,0:T(8,128)S(1)} %bitcast.2) | data formatting | bytes 3145728
